TPU v7x, 32 devices: a whole 2x2x4 slice. The times are simulated.
32 devices in a mesh: pix: 16 (over z, y, x), lat: 2 (over core).
Axes of the slice: x: 2, y: 2, z: 4, core: 2. Of those that a mesh axis runs over, the one named last changes fastest.
Arguments:
- latents: bfloat16 [8192, 512], P('pix'), may hold values from -6 to 6
- w_send: bfloat16 [512, 512], P(None, 'lat'), may hold values from -0.25 to 0.25
- w_recv: bfloat16 [512, 512], P(None, 'lat'), may hold values from -0.25 to 0.25
- edge_bias: float32 [512], P('lat'), may hold values from -3 to 3
- w_msg: bfloat16 [512, 512], P('lat'), may hold values from -0.25 to 0.25
- w_self: bfloat16 [512, 512], P(None, 'lat'), may hold values from -0.25 to 0.25
- w_agg: bfloat16 [512, 512], P(None, 'lat'), may hold values from -0.25 to 0.25
- node_bias: float32 [512], P('lat'), may hold values from -3 to 3
- w_node: bfloat16 [512, 512], P('lat'), may hold values from -0.25 to 0.25
- norm_gain: float32 [512], replicated, may hold values from 0.25 to 1.75
- coarse_ids: int32 [128], P('pix'), may hold values from 0 to 511
- send_list: int32 [16], P('pix'), may hold values from 0 to 3
- recv_tile: int32 [512], P('pix'), may hold values from 0 to 3
- send_tile: int32 [512], P('pix'), may hold values from 0 to 6, as said below
- edge_ends: int32 [512, 2, 128], P('pix'), may hold values from 0 to 127
- edge_mask: int32 [512, 128], P('pix'), may hold values 0 or 1
- cotangent: bfloat16 [8192, 512], P('pix'), may hold values from -6 to 6
Outputs:
- new_latents: bfloat16 [8192, 512], P('pix')
- grad_latents: float32 [8192, 512], P('pix', 'lat')
- grad_w_send: float32 [512, 512], P(None, 'lat')
- grad_w_recv: float32 [512, 512], P(None, 'lat')
- grad_edge_bias: float32 [512], P('lat')
- grad_w_msg: float32 [512, 512], P('lat')
- grad_w_self: float32 [512, 512], P(None, 'lat')
- grad_w_agg: float32 [512, 512], P(None, 'lat')
- grad_node_bias: float32 [512], P('lat')
- grad_w_node: float32 [512, 512], P('lat')
- grad_gain: float32 [512], replicated
Inputs may be any that keep to these rules, and one draw needn't show every extreme that they name: `send_tile`: a block's sender tile, numbered as in the first step: first the device's own tiles, then the 1 lent tiles of the preceding and of the following pixel range, then the 1 tiles of the coarse panel; in each device's own run of 32 blocks, the first names a tile lent by the preceding range and the second one lent by the following range. `coarse_ids`: rows may repeat.
All inputs are finite; a program needn't handle non-finite values. No bound on the sum of `edge_mask` on one device may be relied on, other than what follows from the above.
Results may differ from a plain program's by a relative error of at most 0.0085.
Values may be sent and summed in bfloat16 or wider, within the bound.
A program may use at most 128 MiB of HBM per device.

v0:
```python
import math
import jax
import jax.numpy as jnp
from jax import lax
from jax.sharding import PartitionSpec as P

norm_eps = 1e-05


def from_behind(block, axis, distance):
    devices = range(lax.axis_size(axis))
    route = [((i - distance) % len(devices), i) for i in devices]
    return lax.ppermute(block, axis, route)


def silu_slope(values):
    sigma = jax.nn.sigmoid(values)
    return sigma * (1.0 + values * (1.0 - sigma))


def tile_sums(values, offsets, weights, block_tiles, tile_count):
    block_count, tile_len = offsets.shape
    width = values.shape[-1]
    positions = jnp.arange(tile_len, dtype=jnp.int32)
    incidence = (offsets[:, :, None] == positions[None, None, :]).astype(jnp.float32) * weights[
        :, :, None
    ]
    per_block = jnp.einsum(
        "ben,beh->bnh",
        incidence,
        values.reshape(block_count, tile_len, width),
        precision=lax.Precision.HIGHEST,
    )
    tile_ids = jnp.arange(tile_count, dtype=jnp.int32)
    selector = (block_tiles[None, :] == tile_ids[:, None]).astype(jnp.float32)
    summed = jnp.einsum("tb,bnh->tnh", selector, per_block, precision=lax.Precision.HIGHEST)
    return summed.reshape(tile_count * tile_len, width)


def shards(
    latents,
    w_send,
    w_recv,
    edge_bias,
    w_msg,
    w_self,
    w_agg,
    node_bias,
    w_node,
    norm_gain,
    coarse_ids,
    send_list,
    recv_tile,
    send_tile,
    edge_ends,
    edge_mask,
    cotangent,
):
    node_dev, latent_width = latents.shape
    tile_len = edge_ends.shape[2]
    tiles_dev = node_dev // tile_len
    halo_rows = send_list.shape[0] * tile_len
    pix_count = lax.axis_size("pix")
    lat_count = lax.axis_size("lat")
    grad_scale = 1.0 / math.sqrt(node_dev * pix_count)
    hidden_part = w_send.shape[1]
    send_proj = jnp.dot(latents, w_send, preferred_element_type=jnp.float32)
    recv_proj = jnp.dot(latents, w_recv, preferred_element_type=jnp.float32)
    lent_rows = latents.reshape(tiles_dev, tile_len, latent_width)[send_list].reshape(
        halo_rows, latent_width
    )
    from_left = from_behind(lent_rows, "pix", 1)
    from_right = from_behind(lent_rows, "pix", -1)
    side_proj = jnp.dot(
        jnp.concatenate([from_left, from_right], axis=0), w_send, preferred_element_type=jnp.float32
    )
    panel_proj = jnp.dot(
        lax.all_gather(latents[coarse_ids], "pix", axis=0, tiled=True),
        w_send,
        preferred_element_type=jnp.float32,
    )
    source_proj = jnp.concatenate([send_proj, side_proj, panel_proj], axis=0)
    source_tiles = source_proj.shape[0] // tile_len
    sender_offs = edge_ends[:, 0, :]
    receiver_offs = edge_ends[:, 1, :]
    senders = (send_tile[:, None] * tile_len + sender_offs).reshape(-1)
    receivers = (recv_tile[:, None] * tile_len + receiver_offs).reshape(-1)
    mask_rows = edge_mask.astype(jnp.float32)
    edge_weight = mask_rows.reshape(-1)
    unit_rows = jnp.ones_like(mask_rows)
    edge_pre = source_proj[senders] + recv_proj[receivers] + edge_bias
    edge_act = jax.nn.silu(edge_pre).astype(jnp.bfloat16)
    message = jnp.dot(edge_act, w_msg, preferred_element_type=jnp.float32)
    agg_part = tile_sums(message, receiver_offs, mask_rows, recv_tile, tiles_dev)
    aggregate = lax.psum(agg_part, "lat")
    aggregate_bf = aggregate.astype(jnp.bfloat16)
    node_pre = (
        jnp.dot(latents, w_self, preferred_element_type=jnp.float32)
        + jnp.dot(aggregate_bf, w_agg, preferred_element_type=jnp.float32)
        + node_bias
    )
    node_act = jax.nn.silu(node_pre).astype(jnp.bfloat16)
    out_part = jnp.dot(node_act, w_node, preferred_element_type=jnp.float32)
    node_out = lax.psum(out_part, "lat")
    row_mean = jnp.mean(node_out, axis=-1, keepdims=True)
    centered = node_out - row_mean
    row_var = jnp.mean(centered * centered, axis=-1, keepdims=True)
    inv_std = lax.rsqrt(row_var + norm_eps)
    normed = centered * inv_std
    new_latents = (latents.astype(jnp.float32) + normed * norm_gain).astype(jnp.bfloat16)
    grad_out = cotangent.astype(jnp.float32)
    gain_sum = jnp.sum(grad_out * normed, axis=0)
    d_normed = grad_out * norm_gain
    out_cot = inv_std * (
        d_normed
        - jnp.mean(d_normed, axis=-1, keepdims=True)
        - normed * jnp.mean(d_normed * normed, axis=-1, keepdims=True)
    )
    out_cot_bf = out_cot.astype(jnp.bfloat16)
    node_w_grad = jnp.dot(node_act.T, out_cot_bf, preferred_element_type=jnp.float32)
    node_pre_cot = jnp.dot(out_cot_bf, w_node.T, preferred_element_type=jnp.float32) * silu_slope(
        node_pre
    )
    node_bias_sum = jnp.sum(node_pre_cot, axis=0)
    node_pre_bf = node_pre_cot.astype(jnp.bfloat16)
    self_w_grad = jnp.dot(latents.T, node_pre_bf, preferred_element_type=jnp.float32)
    agg_w_grad = jnp.dot(aggregate_bf.T, node_pre_bf, preferred_element_type=jnp.float32)
    latent_part = jnp.dot(node_pre_bf, w_self.T, preferred_element_type=jnp.float32)
    agg_cot_part = jnp.dot(node_pre_bf, w_agg.T, preferred_element_type=jnp.float32)
    agg_cot = lax.psum(agg_cot_part, "lat")
    agg_cot_bf = agg_cot.astype(jnp.bfloat16)
    msg_cot = agg_cot_bf[receivers] * edge_weight.astype(jnp.bfloat16)[:, None]
    msg_w_grad = jnp.dot(edge_act.T, msg_cot, preferred_element_type=jnp.float32)
    pre_cot = jnp.dot(msg_cot, w_msg.T, preferred_element_type=jnp.float32) * silu_slope(edge_pre)
    edge_bias_sum = jnp.sum(pre_cot, axis=0)
    src_cot = tile_sums(pre_cot, sender_offs, unit_rows, send_tile, source_tiles)
    dst_cot = tile_sums(pre_cot, receiver_offs, unit_rows, recv_tile, tiles_dev)
    own_grad = src_cot[:node_dev]
    left_back = src_cot[node_dev : node_dev + halo_rows]
    right_back = src_cot[node_dev + halo_rows : node_dev + 2 * halo_rows]
    panel_part = src_cot[node_dev + 2 * halo_rows :]
    to_left_owner = from_behind(left_back.astype(jnp.bfloat16), "pix", -1).astype(left_back.dtype)
    to_right_owner = from_behind(right_back.astype(jnp.bfloat16), "pix", 1).astype(right_back.dtype)
    returned = (to_left_owner + to_right_owner).reshape(send_list.shape[0], tile_len, hidden_part)
    own_grad = own_grad.reshape(tiles_dev, tile_len, hidden_part).at[send_list].add(returned)
    own_grad = own_grad.reshape(node_dev, hidden_part)
    coarse_grad = lax.psum_scatter(panel_part, "pix", scatter_dimension=0, tiled=True)
    own_grad = own_grad.at[coarse_ids].add(coarse_grad)
    src_cot_bf = own_grad.astype(jnp.bfloat16)
    dst_cot_bf = dst_cot.astype(jnp.bfloat16)
    send_w_grad = jnp.dot(latents.T, src_cot_bf, preferred_element_type=jnp.float32)
    recv_w_grad = jnp.dot(latents.T, dst_cot_bf, preferred_element_type=jnp.float32)
    latent_part = (
        latent_part
        + jnp.dot(src_cot_bf, w_send.T, preferred_element_type=jnp.float32)
        + jnp.dot(dst_cot_bf, w_recv.T, preferred_element_type=jnp.float32)
    )
    share_width = latent_width // lat_count
    lat_index = lax.axis_index("lat")
    lat_share = lax.psum_scatter(
        latent_part.astype(jnp.bfloat16), "lat", scatter_dimension=1, tiled=True
    ).astype(jnp.float32)
    grad_latents = lat_share + lax.dynamic_slice_in_dim(
        grad_out, lat_index * share_width, share_width, 1
    )
    summed = lax.psum(
        (
            send_w_grad,
            recv_w_grad,
            edge_bias_sum,
            msg_w_grad,
            self_w_grad,
            agg_w_grad,
            node_bias_sum,
            node_w_grad,
            gain_sum,
        ),
        "pix",
    )
    scaled = [grad_scale * entry for entry in summed]
    return (
        new_latents,
        grad_latents,
        scaled[0],
        scaled[1],
        scaled[2],
        scaled[3],
        scaled[4],
        scaled[5],
        scaled[6],
        scaled[7],
        scaled[8],
    )


def solution(mesh):
    return jax.shard_map(
        shards,
        mesh=mesh,
        in_specs=(
            P("pix", None),
            P(None, "lat"),
            P(None, "lat"),
            P("lat"),
            P("lat", None),
            P(None, "lat"),
            P(None, "lat"),
            P("lat"),
            P("lat", None),
            P(),
            P("pix"),
            P("pix"),
            P("pix"),
            P("pix"),
            P("pix", None, None),
            P("pix", None),
            P("pix", None),
        ),
        out_specs=(
            P("pix", None),
            P("pix", "lat"),
            P(None, "lat"),
            P(None, "lat"),
            P("lat"),
            P("lat", None),
            P(None, "lat"),
            P(None, "lat"),
            P("lat"),
            P("lat", None),
            P(),
        ),
        check_vma=False,
    )
```

profile of v0, /device:TPU:0, one launch (start us, length us, event | category | flops | bytes accessed | tf_op | source)
XLA Modules:
  0.0 465.5 jit_solution(5024926762899600851)
XLA Ops:
  8.9 3.0 collective-permute-start
  11.9 4.1 collective-permute-start.1
  18.3 38.1 %all-gather = bf16[128,512]{1,0:T(8,128)(2,1)S(1)} all-gather(bf16[8,512]{1,0:T(8,128)(2,1)S(1)} %gather_fusion), channel_id=2, replica_groups=mesh['pix'=16,'lat'=2] {'pix'}, dimensions={0}, use_global_device_ids=true | all-gather | bytes 139264 | tf_op jit(solution)/shard_map/all_gather | solution.py:78
  64.9 16.1 %gather_fusion.2 = f32[4096,256]{1,0:T(8,128)} fusion(f32[512,256]{1,0:T(8,128)S(1)} %fusion.54, s32[4096]{0:T(1024)S(1)} %broadcast_clamp_fusion), kind=kCustom, calls=%fused_computation.2 | custom fusion | bytes 8404992 | tf_op jit(solution)/shard_map/gather | solution.py:91
  81.3 16.6 %gather_fusion.1 = f32[4096,256]{1,0:T(8,128)} fusion(f32[896,256]{1,0:T(8,128)S(1)} %pad_maximum_fusion, s32[4096]{0:T(1024)S(1)} %broadcast_clamp_fusion.1), kind=kCustom, calls=%fused_computation.1 | custom fusion | bytes 8404992 | tf_op jit(solution)/shard_map/gather | solution.py:91
  97.9 4.9 %multiply_convert_fusion = bf16[4096,256]{1,0:T(8,128)(2,1)S(1)} fusion(f32[256]{0:T(256)S(1)} %copy-done.22, f32[4096,256]{1,0:T(8,128)} %gather_fusion.1, f32[4096,256]{1,0:T(8,128)} %gather_fusion.2), kind=kLoop, calls=%fused_computation.12 | loop fusion | flops 7340032 | bytes 10486784 | tf_op jit(solution)/shard_map/convert_element_type | solution.py:92
  104.2 8.5 %fusion.11 = f32[32,128,512]{2,1,0:T(8,128)S(1)} fusion(f32[32,128,512]{2,1,0:T(8,128)S(1)} %bitcast.85, f32[32,128]{1,0:T(8,128)S(1)} %get-tuple-element.101, s32[32,128]{1,0:T(8,128)S(1)} %bitcast.94), kind=kOutput, calls=%fused_computation.21 | convolution fusion | flops 3222274048 | bytes 16809984 | tf_op jit(solution)/shard_map/ben,beh->bnh/dot_general | solution.py:28
  112.7 7.7 %fusion = f32[4,128,512]{2,0,1:T(4,128)S(1)} fusion(f32[32,128,512]{2,1,0:T(8,128)S(1)} %fusion.11, s32[32]{0:T(128)S(1)} %copy-done.20), kind=kOutput, calls=%fused_computation.5 | convolution fusion | flops 100663424 | bytes 9437312 | tf_op jit(solution)/shard_map/tb,bnh->tnh/dot_general | solution.py:36
  120.8 6.3 %all-reduce.10 = bf16[512,512]{1,0:T(8,128)(2,1)S(1)} all-reduce(f32[512,512]{1,0:T(8,128)S(1)} %bitcast.90), channel_id=1, replica_groups=mesh['pix'=16,'lat'=2] {'lat'}, use_global_device_ids=true, to_apply=%region_0.1 | all-reduce | flops 262144 | bytes 1572864 | tf_op jit(solution)/shard_map/psum | solution.py:95
  129.2 2.2 fusion.45
  132.2 15.1 %all-reduce.7.cloned.1.call-done = f32[512,512]{1,0:T(8,128)} async-done(((f32[512,512]{1,0:T(8,128)}), f32[512,512]{1,0:T(8,128)}) %all-reduce.7.cloned.1.call-update) | async-done | bytes 1048592 | tf_op jit(solution)/shard_map/psum | solution.py:104
  157.8 6.4 %all-reduce.11 = bf16[512,512]{1,0:T(8,128)(2,1)S(1)} all-reduce(f32[512,512]{1,0:T(8,128)S(1)} %fusion.57), channel_id=1, replica_groups=mesh['pix'=16,'lat'=2] {'lat'}, use_global_device_ids=true, to_apply=%region_6.7 | all-reduce | flops 262144 | bytes 1572864 | tf_op jit(solution)/shard_map/psum | solution.py:130
  164.2 17.5 %gather_fusion.3 = bf16[4096,512]{1,0:T(8,128)(2,1)} fusion(bf16[512,512]{1,0:T(8,128)(2,1)S(1)} %all-reduce.11, s32[4096]{0:T(1024)S(1)} %broadcast_clamp_fusion), kind=kCustom, calls=%fused_computation.3 | custom fusion | bytes 8404992 | tf_op jit(solution)/shard_map/gather | solution.py:132
  181.7 5.9 %fusion.50 = (f32[256]{0:T(256)S(1)}, f32[4096,256]{1,0:T(8,128)S(1)}) fusion(f32[256]{0:T(256)S(1)} %copy-done.22, f32[4096,256]{1,0:T(8,128)} %gather_fusion.1, f32[4096,256]{1,0:T(8,128)} %gather_fusion.2, bf16[256,512]{1,0:T(8,128)(2,1)S(1)} %copy-done, bf16[4096,512]{1,0:T(8,128)(2,1)} %gather_fusion.3, bf16[4096]{0:T(1024)(128)(2,1)S(1)} %get-tuple-element.100), kind=kOutput, calls=%fused_computation.107 | convolution fusion | flops 1087373056 | bytes 17049600 | tf_op jit(solution)/shard_map/dot_general | solution.py:134
  187.6 4.4 fusion.13
  192.0 2.7 fusion.14
  194.7 3.8 fusion.49
  198.8 5.5 %collective-permute-start.2 = (bf16[128,256]{1,0:T(8,128)(2,1)S(1)}, bf16[128,256]{1,0:T(8,128)(2,1)S(1)}, u32[]{:S(2)}, u32[]{:S(2)}) collective-permute-start(bf16[128,256]{1,0:T(8,128)(2,1)S(1)} %bitcast.97), channel_id=1, source_target_pairs={{2,0},{4,2},{6,4},{8,6},{10,8},{12,10},{14,12},{16,14},{18,16},{20... | collective-permute-start | bytes 196616 | tf_op jit(solution)/shard_map/ppermute | solution.py:13
  205.5 5.8 %fusion.17 = bf16[4,128,256]{2,0,1:T(4,128)(2,1)S(1)} fusion(f32[32,128,256]{2,1,0:T(8,128)} %fusion.13, s32[32]{0:T(128)S(1)} %copy-done.20), kind=kOutput, calls=%fused_computation.35 | convolution fusion | flops 50462848 | bytes 4456576 | tf_op jit(solution)/shard_map/tb,bnh->tnh/dot_general | solution.py:36
  215.9 4.1 scatter-add.12
  221.2 61.4 %reduce-scatter.3.cloned.1.call-done = f32[8,256]{1,0:T(8,128)} async-done(((f32[128,256]{1,0:T(8,128)}), f32[8,256]{1,0:T(8,128)}) %reduce-scatter.3.cloned.1.call-update) | async-done | bytes 8208 | tf_op jit(solution)/shard_map/reduce_scatter | solution.py:147
  289.5 4.5 fusion.6
  295.3 38.9 %all-reduce = (f32[256]{0:T(256)S(1)}, f32[256]{0:T(256)S(1)}, f32[512]{0:T(512)S(1)}) all-reduce(f32[256]{0:T(256)S(1)} %get-tuple-element.105, f32[256]{0:T(256)S(1)} %get-tuple-element.92, f32[512]{0:T(512)S(1)} %get-tuple-element.78), channel_id=1, replica_groups=mesh['pix'=16,'lat'=2] {'pix'}, use_global_device_ids=true, to_apply=%region_14.15 | all-reduce | flops 1024 | bytes 8192 | tf_op jit(solution)/shard_map/psum | solution.py:166
  337.8 112.8 %all-reduce.9.cloned.1.call-done = (f32[512,256]{0,1:T(8,128)}, f32[512,256]{0,1:T(8,128)}, f32[256,512]{1,0:T(8,128)}, f32[512,256]{0,1:T(8,128)}, f32[512,256]{0,1:T(8,128)}, /*index=5*/f32[256,512]{1,0:T(8,128)}) async-done(((f32[512,256]{0,1:T(8,128)}, f32[512,256]{0,1:T(8,128)}, f32[256,512]{1,0:T(8,128)}, f32[512,256]{0,1:T(8,128)}, f32[512,256]{0,1:T(8,128)}, /*index=5*/f32[256,512]{1,0:T(8,128)}), ...) | async-done | bytes 3145744 | tf_op jit(solution)/shard_map/psum | solution.py:166
  (132 shorter events, 54.0 us)
Async XLA Ops:
  7.2 95.7 %copy-start = (bf16[256,512]{1,0:T(8,128)(2,1)S(1)}, bf16[256,512]{1,0:T(8,128)(2,1)}, u32[]{:S(2)}) copy-start(bf16[256,512]{1,0:T(8,128)(2,1)} %param.23) | copy-start | bytes 786436
  7.2 56.4 %copy-start.1 = (bf16[512,512]{1,0:T(8,128)(2,1)S(1)}, bf16[512,512]{1,0:T(8,128)(2,1)}, u32[]{:S(2)}) copy-start(bf16[512,512]{1,0:T(8,128)(2,1)} %param.19) | copy-start | bytes 1572868
  7.2 140.1 %all-reduce.7.cloned.1.call-start = ((), (), s32[]{:S(2)}) async-start(), calls=%async_computation.2 | async-start | bytes 2097152 | tf_op jit(solution)/shard_map/psum | solution.py:104
  8.9 72.1 %collective-permute-start = (bf16[128,512]{1,0:T(8,128)(2,1)S(1)}, bf16[128,512]{1,0:T(8,128)(2,1)S(1)}, u32[]{:S(2)}, u32[]{:S(2)}) collective-permute-start(bf16[128,512]{1,0:T(8,128)(2,1)S(1)} %dynamic-slice_bitcast_fusion), channel_id=1, source_target_pairs={{30,0},{0,2},{2,4},{4,6},{6,8},{8,10},{10,12},{12,14},{14,16},{16,... | collective-permute-start | bytes 393224 | tf_op jit(solution)/shard_map/ppermute | solution.py:13
  11.9 69.1 %collective-permute-start.1 = (bf16[128,512]{1,0:T(8,128)(2,1)S(1)}, bf16[128,512]{1,0:T(8,128)(2,1)S(1)}, u32[]{:S(2)}, u32[]{:S(2)}) collective-permute-start(bf16[128,512]{1,0:T(8,128)(2,1)S(1)} %dynamic-slice_bitcast_fusion), channel_id=1, source_target_pairs={{2,0},{4,2},{6,4},{8,6},{10,8},{12,10},{14,12},{16,14},{18,16},{20... | collective-permute-start | bytes 393224 | tf_op jit(solution)/shard_map/ppermute | solution.py:13
  64.9 16.1 %copy-start.18 = (s32[32,128]{1,0:T(8,128)S(1)}, s32[32,128]{1,0:T(8,128)}, u32[]{:S(2)}) copy-start(s32[32,128]{1,0:T(8,128)} %param.34) | copy-start | bytes 49156
  64.9 16.1 %copy-start.8 = (bf16[512,256]{1,0:T(8,128)(2,1)S(1)}, bf16[512,256]{1,0:T(8,128)(2,1)}, u32[]{:S(2)}) copy-start(bf16[512,256]{1,0:T(8,128)(2,1)} %param.20) | copy-start | bytes 786436
  81.3 16.6 %copy-start.22 = (f32[256]{0:T(256)S(1)}, f32[256]{0:T(256)}, u32[]{:S(2)}) copy-start(f32[256]{0:T(256)} %param.22) | copy-start | bytes 3076
  104.2 8.5 %copy-start.20 = (s32[32]{0:T(128)S(1)}, s32[32]{0:T(128)}, u32[]{:S(2)}) copy-start(s32[32]{0:T(128)} %param.31) | copy-start | bytes 388
  112.7 14.3 %copy-start.21 = (f32[256]{0:T(256)S(1)}, f32[256]{0:T(256)}, u32[]{:S(2)}) copy-start(f32[256]{0:T(256)} %param.26) | copy-start | bytes 3076
  120.4 11.1 %copy-start.24 = (s32[3]{0:T(128)S(1)}, s32[3]{0:T(128)}, u32[]{:S(2)}) copy-start(s32[3]{0:T(128)} %constant.62.clone.1) | copy-start | bytes 40
  127.1 23.3 %copy-start.5 = (bf16[512,512]{1,0:T(8,128)(2,1)S(1)}, bf16[512,512]{1,0:T(8,128)(2,1)}, u32[]{:S(2)}) copy-start(bf16[512,512]{1,0:T(8,128)(2,1)} %param.35) | copy-start | bytes 1572868
  127.1 23.3 %copy-start.19 = (f32[512]{0:T(512)S(1)}, f32[512]{0:T(512)}, u32[]{:S(2)}) copy-start(f32[512]{0:T(512)} %param.28) | copy-start | bytes 6148
  131.4 22.0 %copy-start.13 = (f32[512,256]{1,0:T(8,128)S(1)}, f32[512,256]{1,0:T(8,128)}, u32[]{:S(2)}) copy-start(f32[512,256]{1,0:T(8,128)} %copy-done.12) | copy-start | bytes 1572868
  131.5 151.1 %reduce-scatter.3.cloned.1.call-start = ((), (), s32[]{:S(2)}) async-start(), calls=%async_computation.3 | async-start | bytes 139264 | tf_op jit(solution)/shard_map/reduce_scatter | solution.py:147
  147.3 4.8 %copy-start.2 = (f32[512,512]{1,0:T(8,128)S(1)}, f32[512,512]{1,0:T(8,128)}, u32[]{:S(2)}) copy-start(f32[512,512]{1,0:T(8,128)} %all-reduce.7.cloned.1.call-done) | copy-start | bytes 3145732
  198.8 15.3 %collective-permute-start.2 = (bf16[128,256]{1,0:T(8,128)(2,1)S(1)}, bf16[128,256]{1,0:T(8,128)(2,1)S(1)}, u32[]{:S(2)}, u32[]{:S(2)}) collective-permute-start(bf16[128,256]{1,0:T(8,128)(2,1)S(1)} %bitcast.97), channel_id=1, source_target_pairs={{2,0},{4,2},{6,4},{8,6},{10,8},{12,10},{14,12},{16,14},{18,16},{20... | collective-permute-start | bytes 196616 | tf_op jit(solution)/shard_map/ppermute | solution.py:13
  204.3 9.7 %collective-permute-start.3 = (bf16[128,256]{1,0:T(8,128)(2,1)S(1)}, bf16[128,256]{1,0:T(8,128)(2,1)S(1)}, u32[]{:S(2)}, u32[]{:S(2)}) collective-permute-start(bf16[128,256]{1,0:T(8,128)(2,1)S(1)} %bitcast.98), channel_id=1, source_target_pairs={{30,0},{0,2},{2,4},{4,6},{6,8},{8,10},{10,12},{12,14},{14,16},{16,... | collective-permute-start | bytes 196616 | tf_op jit(solution)/shard_map/ppermute | solution.py:13
  205.2 130.8 %reduce-scatter.5.cloned.1.call-start = ((), (), s32[]{:S(2)}) async-start(), calls=%async_computation.4 | async-start | bytes 786432 | tf_op jit(solution)/shard_map/reduce_scatter | solution.py:160
  215.9 73.6 %copy-start.4 = (bf16[4096,256]{1,0:T(8,128)(2,1)S(1)}, bf16[4096,256]{1,0:T(8,128)(2,1)}, u32[]{:S(2)}) copy-start(bf16[4096,256]{1,0:T(8,128)(2,1)} %copy-done.3) | copy-start | bytes 6291460
  287.4 163.2 %all-reduce.9.cloned.1.call-start = ((), (), s32[]{:S(2)}) async-start(), calls=%async_computation.5 | async-start | bytes 6291456 | tf_op jit(solution)/shard_map/psum | solution.py:166
  450.6 5.4 %copy-start.16 = (f32[512,256]{0,1:T(8,128)S(1)}, f32[512,256]{0,1:T(8,128)}, u32[]{:S(2)}) copy-start(f32[512,256]{0,1:T(8,128)} %get-tuple-element.88) | copy-start | bytes 1572868
  450.6 6.4 %copy-start.15 = (f32[256,512]{1,0:T(8,128)S(1)}, f32[256,512]{1,0:T(8,128)}, u32[]{:S(2)}) copy-start(f32[256,512]{1,0:T(8,128)} %get-tuple-element.89) | copy-start | bytes 1572868
  451.8 6.1 %copy-start.14 = (f32[256,512]{1,0:T(8,128)S(1)}, f32[256,512]{1,0:T(8,128)}, u32[]{:S(2)}) copy-start(f32[256,512]{1,0:T(8,128)} %get-tuple-element.86) | copy-start | bytes 1572868
  (10 other events, 22.9 us)
Sparse Core Ops, SparseCore 0:
  131.6 15.7 all-reduce.6
  205.3 77.1 reduce-scatter.2
  287.5 4.2 reduce-scatter.4
  299.8 150.6 all-reduce.8
where the time goes:
time: 469 us; the launch traced here: 465 us
  waiting for transfers between devices  189 us (40%)
  blocking collectives  89.7 us (19%)
  local copies, waits for them, and re-layouts  67 us (14%)
  matrix products  65.9 us (14%)
  other arithmetic  25.2 us (5%)
  between operations  15.3 us (3%)
  starting transfers between devices  13 us (3%)
    psum x1, waiting for transfers between devices, shards(): lax.psum((send_w_grad, recv_w_grad, edge_bias_sum, msg_w_grad, self_w_gra...  113 us
    reduce_scatter x1, waiting for transfers between devices, shards(): lax.psum_scatter(panel_part, 'pix', scatter_dimension=0, tiled=True)  61.4 us
    psum x1, blocking collectives, shards(): lax.psum((send_w_grad, recv_w_grad, edge_bias_sum, msg_w_grad, self_w_gra...  38.9 us
    all_gather x1, blocking collectives, shards(): lax.all_gather(latents[coarse_ids], 'pix', axis=0, tiled=True)  38.1 us
    gather x2, local copies, waits for them, and re-layouts, shards(): edge_pre = source_proj[senders] + recv_proj[receivers] + edge_bias  32.7 us
    gather x1, local copies, waits for them, and re-layouts, shards(): msg_cot = agg_cot_bf[receivers] * edge_weight.astype(jnp.bfloat16)[:, None]  17.5 us
    dot_general x3, matrix products, tile_sums(): jnp.einsum('tb,bnh->tnh', selector, per_block, precision=lax.Precision.HI...  17.3 us
    dot_general x3, matrix products, tile_sums(): jnp.einsum('ben,beh->bnh', incidence, values.reshape(block_count, tile_le...  15.6 us
  transfers between devices with their start and end apart: 8, of which 3 were waited for; matrix products, arithmetic and copies ran while one was open for 12% of the time, Pallas kernels for 0%

commit v1 on v0

--- a/solution.py
+++ b/solution.py
@@ -3,6 +3,7 @@
 import jax.numpy as jnp
 from jax import lax
 from jax.sharding import PartitionSpec as P
+from jax.lax import axis_index, axis_size, ppermute
 
 norm_eps = 1e-05
 
@@ -74,10 +75,22 @@
     side_proj = jnp.dot(
         jnp.concatenate([from_left, from_right], axis=0), w_send, preferred_element_type=jnp.float32
     )
+
+    def return_all_knots(work_x):
+        u1, y_new = (axis_size("pix"), axis_index("pix"))
+        mixed_arr, v_now = (work_x, 1)
+        while v_now < u1:
+            outcome_arr = ppermute(
+                mixed_arr, axis_name="pix", perm=[(no, no ^ v_now) for no in range(u1)]
+            )
+            tmp = jnp.concatenate([mixed_arr, outcome_arr], axis=0)
+            u_next = jnp.concatenate([outcome_arr, mixed_arr], axis=0)
+            mixed_arr = jnp.where(y_new & v_now == 0, tmp, u_next)
+            v_now = 2 * v_now
+        return mixed_arr
+
     panel_proj = jnp.dot(
-        lax.all_gather(latents[coarse_ids], "pix", axis=0, tiled=True),
-        w_send,
-        preferred_element_type=jnp.float32,
+        return_all_knots(latents[coarse_ids]), w_send, preferred_element_type=jnp.float32
     )
     source_proj = jnp.concatenate([send_proj, side_proj, panel_proj], axis=0)
     source_tiles = source_proj.shape[0] // tile_len

time: 469 us -> 439 us (0.936)
  blocking collectives: 89.7 us -> 51.4 us
  waiting for transfers between devices: 189 us -> 200 us
    all_gather x1 -> x0, blocking collectives: 38.1 us -> none  [shards(): lax.all_gather(latents[coarse_ids], 'pix', axis=0, tiled=True)]
    ppermute x0 -> x4, waiting for transfers between devices: none -> 7.59 us  [return_all_knots(): ppermute(mixed_arr, axis_name='pix', perm=[(no, no ^ v_now) for no in ran...]
  transfers between devices with their start and end apart: 8 -> 12, of which waited for: 3 -> 5; matrix products, arithmetic and copies ran while one was open for 12% -> 12% of each run, Pallas kernels for 0% -> 0%
where the time goes in v1:
time: 439 us; the launch traced here: 435 us
  waiting for transfers between devices  200 us (46%)
  local copies, waits for them, and re-layouts  65.3 us (15%)
  matrix products  64.3 us (15%)
  blocking collectives  51.4 us (12%)
  other arithmetic  24.4 us (6%)
  between operations  15.4 us (4%)
  starting transfers between devices  14.2 us (3%)
    psum x1, waiting for transfers between devices, shards(): lax.psum((send_w_grad, recv_w_grad, edge_bias_sum, msg_w_grad, self_w_gra...  113 us
    reduce_scatter x1, waiting for transfers between devices, shards(): lax.psum_scatter(panel_part, 'pix', scatter_dimension=0, tiled=True)  61.4 us
    psum x1, blocking collectives, shards(): lax.psum((send_w_grad, recv_w_grad, edge_bias_sum, msg_w_grad, self_w_gra...  38.7 us
    gather x2, local copies, waits for them, and re-layouts, shards(): edge_pre = source_proj[senders] + recv_proj[receivers] + edge_bias  32.6 us
    psum x1, waiting for transfers between devices, shards(): node_out = lax.psum(out_part, 'lat')  18.3 us
    gather x1, local copies, waits for them, and re-layouts, shards(): msg_cot = agg_cot_bf[receivers] * edge_weight.astype(jnp.bfloat16)[:, None]  17.5 us
    dot_general x3, matrix products, tile_sums(): jnp.einsum('tb,bnh->tnh', selector, per_block, precision=lax.Precision.HI...  17.3 us
    dot_general x3, matrix products, tile_sums(): jnp.einsum('ben,beh->bnh', incidence, values.reshape(block_count, tile_le...  15.6 us
  transfers between devices with their start and end apart: 12, of which 5 were waited for; matrix products, arithmetic and copies ran while one was open for 12% of the time, Pallas kernels for 0%

profile of v1, /device:TPU:0, one launch (start us, length us, event | category | flops | bytes accessed | tf_op | source)
XLA Modules:
  0.0 435.4 jit_solution(10392561790696740265)
XLA Ops:
  8.9 3.0 collective-permute-start
  11.9 4.1 collective-permute-start.1
  24.3 3.7 collective-permute-done.3
  28.1 3.9 collective-permute-done.4
  32.9 16.1 %gather_fusion.2 = f32[4096,256]{1,0:T(8,128)} fusion(f32[512,256]{1,0:T(8,128)S(1)} %fusion.61, s32[4096]{0:T(1024)S(1)} %broadcast_clamp_fusion), kind=kCustom, calls=%fused_computation.2 | custom fusion | bytes 8404992 | tf_op jit(solution)/shard_map/gather | solution.py:104
  49.5 16.6 %gather_fusion.1 = f32[4096,256]{1,0:T(8,128)} fusion(f32[896,256]{1,0:T(8,128)S(1)} %pad_maximum_fusion, s32[4096]{0:T(1024)S(1)} %broadcast_clamp_fusion.1), kind=kCustom, calls=%fused_computation.1 | custom fusion | bytes 8404992 | tf_op jit(solution)/shard_map/gather | solution.py:104
  66.1 4.9 %multiply_convert_fusion = bf16[4096,256]{1,0:T(8,128)(2,1)S(1)} fusion(f32[256]{0:T(256)S(1)} %copy-done.24, f32[4096,256]{1,0:T(8,128)} %gather_fusion.1, f32[4096,256]{1,0:T(8,128)} %gather_fusion.2), kind=kLoop, calls=%fused_computation.12 | loop fusion | flops 7340032 | bytes 10486784 | tf_op jit(solution)/shard_map/convert_element_type | solution.py:105
  72.4 8.5 %fusion.11 = f32[32,128,512]{2,1,0:T(8,128)S(1)} fusion(f32[32,128,512]{2,1,0:T(8,128)S(1)} %bitcast.84, f32[32,128]{1,0:T(8,128)S(1)} %get-tuple-element.101, s32[32,128]{1,0:T(8,128)S(1)} %bitcast.93), kind=kOutput, calls=%fused_computation.21 | convolution fusion | flops 3222274048 | bytes 16809984 | tf_op jit(solution)/shard_map/ben,beh->bnh/dot_general | solution.py:29
  80.9 7.7 %fusion = f32[4,128,512]{2,0,1:T(4,128)S(1)} fusion(f32[32,128,512]{2,1,0:T(8,128)S(1)} %fusion.11, s32[32]{0:T(128)S(1)} %copy-done.22), kind=kOutput, calls=%fused_computation.5 | convolution fusion | flops 100663424 | bytes 9437312 | tf_op jit(solution)/shard_map/tb,bnh->tnh/dot_general | solution.py:37
  89.0 6.3 %all-reduce.10 = bf16[512,512]{1,0:T(8,128)(2,1)S(1)} all-reduce(f32[512,512]{1,0:T(8,128)S(1)} %bitcast.89), channel_id=1, replica_groups=mesh['pix'=16,'lat'=2] {'lat'}, use_global_device_ids=true, to_apply=%region_0.1 | all-reduce | flops 262144 | bytes 1572864 | tf_op jit(solution)/shard_map/psum | solution.py:108
  98.8 18.3 %all-reduce.7.cloned.1.call-done = f32[512,512]{1,0:T(8,128)} async-done(((f32[512,512]{1,0:T(8,128)}), f32[512,512]{1,0:T(8,128)}) %all-reduce.7.cloned.1.call-update) | async-done | bytes 1048592 | tf_op jit(solution)/shard_map/psum | solution.py:117
  127.7 6.3 %all-reduce.11 = bf16[512,512]{1,0:T(8,128)(2,1)S(1)} all-reduce(f32[512,512]{1,0:T(8,128)S(1)} %fusion.64), channel_id=1, replica_groups=mesh['pix'=16,'lat'=2] {'lat'}, use_global_device_ids=true, to_apply=%region_6.7 | all-reduce | flops 262144 | bytes 1572864 | tf_op jit(solution)/shard_map/psum | solution.py:143
  134.0 17.5 %gather_fusion.3 = bf16[4096,512]{1,0:T(8,128)(2,1)} fusion(bf16[512,512]{1,0:T(8,128)(2,1)S(1)} %all-reduce.11, s32[4096]{0:T(1024)S(1)} %broadcast_clamp_fusion), kind=kCustom, calls=%fused_computation.3 | custom fusion | bytes 8404992 | tf_op jit(solution)/shard_map/gather | solution.py:145
  151.5 5.9 %fusion.58 = (f32[256]{0:T(256)S(1)}, f32[4096,256]{1,0:T(8,128)S(1)}) fusion(f32[256]{0:T(256)S(1)} %copy-done.24, f32[4096,256]{1,0:T(8,128)} %gather_fusion.1, f32[4096,256]{1,0:T(8,128)} %gather_fusion.2, bf16[256,512]{1,0:T(8,128)(2,1)S(1)} %copy-done, bf16[4096,512]{1,0:T(8,128)(2,1)} %gather_fusion.3, bf16[4096]{0:T(1024)(128)(2,1)S(1)} %get-tuple-element.100), kind=kOutput, calls=%fused_computation.119 | convolution fusion | flops 1087373056 | bytes 17049600 | tf_op jit(solution)/shard_map/dot_general | solution.py:147
  157.4 4.4 %fusion.13 = f32[32,128,256]{2,1,0:T(8,128)} fusion(f32[32,128,256]{2,1,0:T(8,128)S(1)} %bitcast.86, s32[32,128]{1,0:T(8,128)S(1)} %bitcast.94), kind=kOutput, calls=%fused_computation.24 | convolution fusion | flops 1611137024 | bytes 8404992 | tf_op jit(solution)/shard_map/ben,beh->bnh/dot_general | solution.py:29
  161.8 2.7 fusion.14
  164.5 3.8 fusion.57
  168.6 5.5 %collective-permute-start.6 = (bf16[128,256]{1,0:T(8,128)(2,1)S(1)}, bf16[128,256]{1,0:T(8,128)(2,1)S(1)}, u32[]{:S(2)}, u32[]{:S(2)}) collective-permute-start(bf16[128,256]{1,0:T(8,128)(2,1)S(1)} %bitcast.96), channel_id=1, source_target_pairs={{2,0},{4,2},{6,4},{8,6},{10,8},{12,10},{14,12},{16,14},{18,16},{20... | collective-permute-start | bytes 196616 | tf_op jit(solution)/shard_map/ppermute | solution.py:14
  175.3 5.8 %fusion.17 = bf16[4,128,256]{2,0,1:T(4,128)(2,1)S(1)} fusion(f32[32,128,256]{2,1,0:T(8,128)} %fusion.13, s32[32]{0:T(128)S(1)} %copy-done.22), kind=kOutput, calls=%fused_computation.35 | convolution fusion | flops 50462848 | bytes 4456576 | tf_op jit(solution)/shard_map/tb,bnh->tnh/dot_general | solution.py:37
  185.8 4.1 scatter-add.12
  191.0 61.4 %reduce-scatter.3.cloned.1.call-done = f32[8,256]{1,0:T(8,128)} async-done(((f32[128,256]{1,0:T(8,128)}), f32[8,256]{1,0:T(8,128)}) %reduce-scatter.3.cloned.1.call-update) | async-done | bytes 8208 | tf_op jit(solution)/shard_map/reduce_scatter | solution.py:160
  259.4 4.5 %fusion.6 = f32[256,512]{1,0:T(8,128)} fusion(bf16[4096,256]{1,0:T(8,128)(2,1)S(1)} %copy-done.4, bf16[4096,512]{1,0:T(8,128)(2,1)} %gather_fusion.3, bf16[4096]{0:T(1024)(128)(2,1)S(1)} %get-tuple-element.100), kind=kOutput, calls=%fused_computation.15 | convolution fusion | flops 1075838976 | bytes 6823936 | tf_op jit(solution)/shard_map/dot_general | solution.py:146
  265.2 38.7 %all-reduce = (f32[256]{0:T(256)S(1)}, f32[256]{0:T(256)S(1)}, f32[512]{0:T(512)S(1)}) all-reduce(f32[256]{0:T(256)S(1)} %get-tuple-element.105, f32[256]{0:T(256)S(1)} %get-tuple-element.92, f32[512]{0:T(512)S(1)} %get-tuple-element.78), channel_id=1, replica_groups=mesh['pix'=16,'lat'=2] {'pix'}, use_global_device_ids=true, to_apply=%region_14.15 | all-reduce | flops 1024 | bytes 8192 | tf_op jit(solution)/shard_map/psum | solution.py:179
  307.5 113.0 %all-reduce.9.cloned.1.call-done = (f32[512,256]{0,1:T(8,128)}, f32[512,256]{0,1:T(8,128)}, f32[256,512]{1,0:T(8,128)}, f32[512,256]{0,1:T(8,128)}, f32[512,256]{0,1:T(8,128)}, /*index=5*/f32[256,512]{1,0:T(8,128)}) async-done(((f32[512,256]{0,1:T(8,128)}, f32[512,256]{0,1:T(8,128)}, f32[256,512]{1,0:T(8,128)}, f32[512,256]{0,1:T(8,128)}, f32[512,256]{0,1:T(8,128)}, /*index=5*/f32[256,512]{1,0:T(8,128)}), ...) | async-done | bytes 3145744 | tf_op jit(solution)/shard_map/psum | solution.py:179
  (146 shorter events, 53.4 us)
Async XLA Ops:
  7.2 63.8 %copy-start = (bf16[256,512]{1,0:T(8,128)(2,1)S(1)}, bf16[256,512]{1,0:T(8,128)(2,1)}, u32[]{:S(2)}) copy-start(bf16[256,512]{1,0:T(8,128)(2,1)} %param.23) | copy-start | bytes 786436
  7.2 16.8 %copy-start.19 = (s32[32,2,128]{2,1,0:T(2,128)S(1)}, s32[32,2,128]{2,1,0:T(2,128)}, u32[]{:S(2)}) copy-start(s32[32,2,128]{2,1,0:T(2,128)} %param.33) | copy-start | bytes 98308
  7.2 25.7 %copy-start.20 = (s32[32,128]{1,0:T(8,128)S(1)}, s32[32,128]{1,0:T(8,128)}, u32[]{:S(2)}) copy-start(s32[32,128]{1,0:T(8,128)} %param.34) | copy-start | bytes 49156
  7.2 109.9 %all-reduce.7.cloned.1.call-start = ((), (), s32[]{:S(2)}) async-start(), calls=%async_computation.2 | async-start | bytes 2097152 | tf_op jit(solution)/shard_map/psum | solution.py:117
  8.9 40.3 %collective-permute-start = (bf16[128,512]{1,0:T(8,128)(2,1)S(1)}, bf16[128,512]{1,0:T(8,128)(2,1)S(1)}, u32[]{:S(2)}, u32[]{:S(2)}) collective-permute-start(bf16[128,512]{1,0:T(8,128)(2,1)S(1)} %dynamic-slice_bitcast_fusion), channel_id=1, source_target_pairs={{30,0},{0,2},{2,4},{4,6},{6,8},{8,10},{10,12},{12,14},{14,16},{16,... | collective-permute-start | bytes 393224 | tf_op jit(solution)/shard_map/ppermute | solution.py:14
  11.9 37.4 %collective-permute-start.1 = (bf16[128,512]{1,0:T(8,128)(2,1)S(1)}, bf16[128,512]{1,0:T(8,128)(2,1)S(1)}, u32[]{:S(2)}, u32[]{:S(2)}) collective-permute-start(bf16[128,512]{1,0:T(8,128)(2,1)S(1)} %dynamic-slice_bitcast_fusion), channel_id=1, source_target_pairs={{2,0},{4,2},{6,4},{8,6},{10,8},{12,10},{14,12},{16,14},{18,16},{20... | collective-permute-start | bytes 393224 | tf_op jit(solution)/shard_map/ppermute | solution.py:14
  18.3 5.9 %collective-permute-start.2 = (bf16[8,512]{1,0:T(8,128)(2,1)S(1)}, bf16[8,512]{1,0:T(8,128)(2,1)S(1)}, u32[]{:S(2)}, u32[]{:S(2)}) collective-permute-start(bf16[8,512]{1,0:T(8,128)(2,1)S(1)} %gather_fusion), channel_id=1, source_target_pairs={{0,2},{2,0},{4,6},{6,4},{8,10},{10,8},{12,14},{14,12},{16,18},{18,... | collective-permute-start | bytes 24584 | tf_op jit(solution)/shard_map/ppermute | solution.py:83
  24.2 3.8 collective-permute-start.3
  28.0 4.0 collective-permute-start.4
  32.0 17.0 %collective-permute-start.5 = (bf16[64,512]{1,0:T(8,128)(2,1)S(1)}, bf16[64,512]{1,0:T(8,128)(2,1)S(1)}, u32[]{:S(2)}, u32[]{:S(2)}) collective-permute-start(bf16[64,512]{1,0:T(8,128)(2,1)S(1)} %maximum_select_fusion.2), channel_id=1, source_target_pairs={{0,16},{2,18},{4,20},{6,22},{8,24},{10,26},{12,28},{14,30},{16,0},... | collective-permute-start | bytes 196616 | tf_op jit(solution)/shard_map/ppermute | solution.py:83
  32.9 16.1 %copy-start.8 = (bf16[512,256]{1,0:T(8,128)(2,1)S(1)}, bf16[512,256]{1,0:T(8,128)(2,1)}, u32[]{:S(2)}) copy-start(bf16[512,256]{1,0:T(8,128)(2,1)} %param.20) | copy-start | bytes 786436
  49.5 16.6 %copy-start.24 = (f32[256]{0:T(256)S(1)}, f32[256]{0:T(256)}, u32[]{:S(2)}) copy-start(f32[256]{0:T(256)} %param.22) | copy-start | bytes 3076
  80.9 14.4 %copy-start.10 = (bf16[512,256]{1,0:T(8,128)(2,1)S(1)}, bf16[512,256]{1,0:T(8,128)(2,1)}, u32[]{:S(2)}) copy-start(bf16[512,256]{1,0:T(8,128)(2,1)} %param.25) | copy-start | bytes 786436
  80.9 14.4 %copy-start.23 = (f32[256]{0:T(256)S(1)}, f32[256]{0:T(256)}, u32[]{:S(2)}) copy-start(f32[256]{0:T(256)} %param.26) | copy-start | bytes 3076
  88.6 9.5 %copy-start.26 = (s32[3]{0:T(128)S(1)}, s32[3]{0:T(128)}, u32[]{:S(2)}) copy-start(s32[3]{0:T(128)} %constant.75.clone.1) | copy-start | bytes 40
  95.3 24.9 %copy-start.5 = (bf16[512,512]{1,0:T(8,128)(2,1)S(1)}, bf16[512,512]{1,0:T(8,128)(2,1)}, u32[]{:S(2)}) copy-start(bf16[512,512]{1,0:T(8,128)(2,1)} %param.35) | copy-start | bytes 1572868
  95.3 24.9 %copy-start.21 = (f32[512]{0:T(512)S(1)}, f32[512]{0:T(512)}, u32[]{:S(2)}) copy-start(f32[512]{0:T(512)} %param.28) | copy-start | bytes 6148
  95.3 26.7 %copy-start.1 = (bf16[512,512]{1,0:T(8,128)(2,1)S(1)}, bf16[512,512]{1,0:T(8,128)(2,1)}, u32[]{:S(2)}) copy-start(bf16[512,512]{1,0:T(8,128)(2,1)} %param.19) | copy-start | bytes 1572868
  98.1 154.4 %reduce-scatter.3.cloned.1.call-start = ((), (), s32[]{:S(2)}) async-start(), calls=%async_computation.3 | async-start | bytes 139264 | tf_op jit(solution)/shard_map/reduce_scatter | solution.py:160
  168.6 15.3 %collective-permute-start.6 = (bf16[128,256]{1,0:T(8,128)(2,1)S(1)}, bf16[128,256]{1,0:T(8,128)(2,1)S(1)}, u32[]{:S(2)}, u32[]{:S(2)}) collective-permute-start(bf16[128,256]{1,0:T(8,128)(2,1)S(1)} %bitcast.96), channel_id=1, source_target_pairs={{2,0},{4,2},{6,4},{8,6},{10,8},{12,10},{14,12},{16,14},{18,16},{20... | collective-permute-start | bytes 196616 | tf_op jit(solution)/shard_map/ppermute | solution.py:14
  174.1 9.7 %collective-permute-start.7 = (bf16[128,256]{1,0:T(8,128)(2,1)S(1)}, bf16[128,256]{1,0:T(8,128)(2,1)S(1)}, u32[]{:S(2)}, u32[]{:S(2)}) collective-permute-start(bf16[128,256]{1,0:T(8,128)(2,1)S(1)} %bitcast.97), channel_id=1, source_target_pairs={{30,0},{0,2},{2,4},{4,6},{6,8},{8,10},{10,12},{12,14},{14,16},{16,... | collective-permute-start | bytes 196616 | tf_op jit(solution)/shard_map/ppermute | solution.py:14
  175.0 130.6 %reduce-scatter.5.cloned.1.call-start = ((), (), s32[]{:S(2)}) async-start(), calls=%async_computation.4 | async-start | bytes 786432 | tf_op jit(solution)/shard_map/reduce_scatter | solution.py:173
  185.8 73.6 %copy-start.4 = (bf16[4096,256]{1,0:T(8,128)(2,1)S(1)}, bf16[4096,256]{1,0:T(8,128)(2,1)}, u32[]{:S(2)}) copy-start(bf16[4096,256]{1,0:T(8,128)(2,1)} %copy-done.3) | copy-start | bytes 6291460
  257.3 163.2 %all-reduce.9.cloned.1.call-start = ((), (), s32[]{:S(2)}) async-start(), calls=%async_computation.5 | async-start | bytes 6291456 | tf_op jit(solution)/shard_map/psum | solution.py:179
  (16 other events, 62.9 us)
Sparse Core Ops, SparseCore 0:
  98.2 18.8 all-reduce.6
  175.2 77.2 reduce-scatter.2
  257.4 4.2 reduce-scatter.4
  269.7 150.6 all-reduce.8
